TPU v7x, 512 devices: a whole 4x8x8 slice. The times are simulated.
512 devices in a mesh: dp: 8 (over z), expert: 64 (over y, x, core).
Axes of the slice: x: 4, y: 8, z: 8, core: 2. Of those that a mesh axis runs over, the one named last changes fastest.
Arguments:
- tokens: bfloat16 [65536, 3584], P(('dp', 'expert')), may hold values from -6 to 6
- cotangent: bfloat16 [65536, 3584], P(('dp', 'expert')), may hold values from -6 to 6
- route_ids: int32 [65536, 8], P(('dp', 'expert')), may hold values from 0 to 255, as said below
- route_gates: float32 [65536, 8], P(('dp', 'expert')), may hold values from 0.1 to 1
- gate_w: bfloat16 [3584, 8192], P('dp', 'expert'), may hold values from -0.09375 to 0.09375
- up_w: bfloat16 [3584, 8192], P('dp', 'expert'), may hold values from -0.09375 to 0.09375
- down_w: bfloat16 [3584, 8192], P('dp', 'expert'), may hold values from -0.1875 to 0.1875
Outputs:
- moe_out: bfloat16 [65536, 3584], P(('dp', 'expert'))
- d_tokens: bfloat16 [65536, 3584], P(('dp', 'expert'))
- d_gates: float32 [65536, 8], P(('dp', 'expert'))
- d_gate_w: bfloat16 [3584, 8192], P('dp', 'expert')
- d_up_w: bfloat16 [3584, 8192], P('dp', 'expert')
- d_down_w: bfloat16 [3584, 8192], P('dp', 'expert')
Inputs may be any that keep to these rules, and one draw needn't show every extreme that they name: `route_ids`: each token names 8 different experts; the experts in flight are 0 to 7. Among the tokens of one device (aligned blocks of 128 tokens) each expert in flight is named by at most 6 tokens, and in every draw one expert in flight is named by exactly 6 tokens in every block.
All inputs are finite; a program needn't handle non-finite values.
Results may differ from a plain program's by a relative error of at most 0.017.
Values may be sent and summed in bfloat16 or wider, within the bound.
A program may use at most 64 MiB of HBM per device.

v0:
```python
import jax
import jax.numpy as jnp
from jax import lax
from jax.sharding import PartitionSpec as P

TOP = 8
SLICES = 8
CAP = 6


def shards(tokens, cotangent, route_ids, route_gates, gate_w, up_w, down_w):
    owners = lax.axis_size("expert")
    groups = owners // SLICES
    tok_rows = tokens.shape[0]
    routes = tok_rows * TOP
    flat_ids = route_ids.reshape(routes)
    matched = (flat_ids[:, None] == jnp.arange(groups, dtype=jnp.int32)[None, :]).astype(jnp.int32)
    slot_index = jnp.cumsum(matched, axis=0) - 1
    chosen = (matched[:, :, None] == 1) & (
        slot_index[:, :, None] == jnp.arange(CAP, dtype=jnp.int32)[None, None, :]
    )
    select = jnp.transpose(chosen, (1, 2, 0)).reshape(groups * CAP, routes).astype(jnp.float32)
    tok_select = jnp.sum(select.reshape(groups * CAP, tok_rows, TOP), axis=2)
    slot_gate = jnp.sum(select * route_gates.reshape(routes)[None, :], axis=1)
    pick_rows = tok_select.astype(jnp.bfloat16)
    token_slots = jnp.dot(pick_rows, tokens, preferred_element_type=jnp.float32).astype(
        jnp.bfloat16
    )
    cotangent_slots = jnp.dot(pick_rows, cotangent, preferred_element_type=jnp.float32).astype(
        jnp.bfloat16
    )
    scaled_slots = (slot_gate[:, None] * cotangent_slots.astype(jnp.float32)).astype(jnp.bfloat16)

    def spread(slot_rows):
        width = slot_rows.shape[1]
        grouped = slot_rows.reshape(groups, 1, CAP, width)
        return jnp.broadcast_to(grouped, (groups, SLICES, CAP, width)).reshape(owners * CAP, width)

    w_gate, w_up, w_down = (
        lax.all_gather(gate_w, "dp", axis=0, tiled=True),
        lax.all_gather(up_w, "dp", axis=0, tiled=True),
        lax.all_gather(down_w, "dp", axis=0, tiled=True),
    )
    token_rows = lax.all_to_all(
        spread(token_slots), "expert", split_axis=0, concat_axis=0, tiled=True
    )
    gate_pre = jnp.dot(token_rows, w_gate, preferred_element_type=jnp.float32)
    up_pre = jnp.dot(token_rows, w_up, preferred_element_type=jnp.float32)
    sigmoid_gate = jax.nn.sigmoid(gate_pre)
    active = gate_pre * sigmoid_gate
    hidden = (active * up_pre).astype(jnp.bfloat16)
    contract_cols = (((1,), (1,)), ((), ()))
    out_part = lax.dot_general(
        hidden, w_down, contract_cols, preferred_element_type=jnp.float32
    ).astype(jnp.bfloat16)
    out_back = lax.all_to_all(out_part, "expert", split_axis=0, concat_axis=0, tiled=True)
    scaled_rows = lax.all_to_all(
        spread(scaled_slots), "expert", split_axis=0, concat_axis=0, tiled=True
    )
    d_hidden = jnp.dot(scaled_rows, w_down, preferred_element_type=jnp.float32)
    d_gate_pre = (
        d_hidden * up_pre * sigmoid_gate * (1.0 + gate_pre * (1.0 - sigmoid_gate))
    ).astype(jnp.bfloat16)
    d_up_pre = (d_hidden * active).astype(jnp.bfloat16)
    dx_part = lax.dot_general(d_gate_pre, w_gate, contract_cols, preferred_element_type=jnp.float32)
    dx_part = (
        dx_part + lax.dot_general(d_up_pre, w_up, contract_cols, preferred_element_type=jnp.float32)
    ).astype(jnp.bfloat16)
    contract_rows = (((0,), (0,)), ((), ()))
    gate_term = lax.dot_general(
        token_rows, d_gate_pre, contract_rows, preferred_element_type=jnp.float32
    )
    up_term = lax.dot_general(
        token_rows, d_up_pre, contract_rows, preferred_element_type=jnp.float32
    )
    down_term = lax.dot_general(
        scaled_rows, hidden, contract_rows, preferred_element_type=jnp.float32
    )
    summed_grads = lax.psum_scatter(
        jnp.concatenate([gate_term, up_term, down_term], axis=1).astype(jnp.bfloat16),
        "dp",
        scatter_dimension=0,
        tiled=True,
    ).astype(jnp.float32)
    hidden_cols = gate_w.shape[1]
    d_gate_w = summed_grads[:, :hidden_cols].astype(jnp.bfloat16)
    d_up_w = summed_grads[:, hidden_cols : 2 * hidden_cols].astype(jnp.bfloat16)
    d_down_w = summed_grads[:, 2 * hidden_cols :].astype(jnp.bfloat16)
    dx_back = lax.all_to_all(dx_part, "expert", split_axis=0, concat_axis=0, tiled=True)
    member_wide = spread(tok_select)
    weighted_wide = spread(tok_select * slot_gate[:, None])
    weight_high = weighted_wide.astype(jnp.bfloat16)
    weight_low = (weighted_wide - weight_high.astype(jnp.float32)).astype(jnp.bfloat16)
    moe_sum = lax.dot_general(
        weight_high, out_back, contract_rows, preferred_element_type=jnp.float32
    )
    moe_sum = moe_sum + lax.dot_general(
        weight_low, out_back, contract_rows, preferred_element_type=jnp.float32
    )
    moe_out = moe_sum.astype(jnp.bfloat16)
    d_tokens = lax.dot_general(
        member_wide.astype(jnp.bfloat16), dx_back, contract_rows, preferred_element_type=jnp.float32
    ).astype(jnp.bfloat16)
    inner = lax.dot_general(cotangent, out_back, contract_cols, preferred_element_type=jnp.float32)
    wide_grad = jnp.sum(inner * jnp.transpose(member_wide), axis=0)
    slot_grad = jnp.sum(wide_grad.reshape(groups, SLICES, CAP), axis=1).reshape(groups * CAP)
    d_gates = jnp.sum(slot_grad[:, None] * select, axis=0).reshape(tok_rows, TOP)
    return (moe_out, d_tokens, d_gates, d_gate_w, d_up_w, d_down_w)


def solution(mesh):
    return jax.shard_map(
        shards,
        mesh=mesh,
        in_specs=(
            P(("dp", "expert"), None),
            P(("dp", "expert"), None),
            P(("dp", "expert"), None),
            P(("dp", "expert"), None),
            P("dp", "expert"),
            P("dp", "expert"),
            P("dp", "expert"),
        ),
        out_specs=(
            P(("dp", "expert"), None),
            P(("dp", "expert"), None),
            P(("dp", "expert"), None),
            P("dp", "expert"),
            P("dp", "expert"),
            P("dp", "expert"),
        ),
        check_vma=False,
    )
```

profile of v0, /device:TPU:2, one launch (start us, length us, event | category | flops | bytes accessed | tf_op | source)
XLA Modules:
  0.0 461.1 jit_solution(1026153735217437292)
XLA Ops:
  7.2 0.9 copy.27
  8.4 2.3 reduce-window.6
  10.6 0.3 slice_reduce_fusion
  10.9 0.2 reduce-window.9
  11.2 1.9 and.18
  13.2 3.4 eq.81
  16.6 2.9 convert_reduce_fusion
  19.6 0.3 convolution_convert_fusion.6
  19.9 2.1 broadcast_in_dim.36
  22.1 11.0 %all-to-all-start = ((bf16[64,6,3584]{2,1,0:T(8,128)(2,1)}), bf16[64,6,3584]{2,1,0:T(8,128)(2,1)}, u32[]{:S(2)}, u32[]{:S(2)}) async-start(bf16[64,6,3584]{2,1,0:T(8,128)(2,1)} %bitcast.37), calls=%async_computation | async-start | bytes 7340032 | tf_op jit(solution)/shard_map/all_to_all | solution.py:44
  33.1 32.2 %all_gather.9 = bf16[3584,128]{1,0:T(8,128)(2,1)S(1)} all-gather(bf16[448,128]{1,0:T(8,128)(2,1)S(1)} %copy-done.10), channel_id=1, replica_groups=mesh['dp'=8,'expert'=64] {'dp'}, dimensions={0}, use_global_device_ids=true | all-gather | bytes 1032192 | tf_op jit(solution)/shard_map/all_gather | solution.py:40
  65.3 26.5 %all_gather.10 = bf16[3584,128]{1,0:T(8,128)(2,1)S(1)} all-gather(bf16[448,128]{1,0:T(8,128)(2,1)S(1)} %copy-done.11), channel_id=1, replica_groups=mesh['dp'=8,'expert'=64] {'dp'}, dimensions={0}, use_global_device_ids=true | all-gather | bytes 1032192 | tf_op jit(solution)/shard_map/all_gather | solution.py:41
  91.8 28.6 %all_gather.11 = bf16[3584,128]{1,0:T(8,128)(2,1)} all-gather(bf16[448,128]{1,0:T(8,128)(2,1)S(1)} %copy-done.12), channel_id=1, replica_groups=mesh['dp'=8,'expert'=64] {'dp'}, dimensions={0}, use_global_device_ids=true | all-gather | bytes 1032192 | tf_op jit(solution)/shard_map/all_gather | solution.py:42
  120.4 5.5 %all_to_all.34 = bf16[384,3584]{1,0:T(8,128)(2,1)} reshape(bf16[64,6,3584]{2,1,0:T(8,128)(2,1)} %all-to-all-done) | data formatting | bytes 5505024 | tf_op jit(solution)/shard_map/all_to_all | solution.py:44
  125.8 2.8 fusion.12
  128.7 0.9 multiply_convert_fusion.2
  129.6 0.3 copy-done.7
  129.8 2.5 convolution_convert_fusion
  132.3 5.4 %all_to_all.35 = bf16[64,6,3584]{2,1,0:T(8,128)(2,1)} reshape(bf16[384,3584]{1,0:T(8,128)(2,1)} %convolution_convert_fusion) | data formatting | bytes 5505024 | tf_op jit(solution)/shard_map/all_to_all | solution.py:56
  137.7 10.1 %all-to-all-start.1 = ((bf16[64,6,3584]{2,1,0:T(8,128)(2,1)}), bf16[64,6,3584]{2,1,0:T(8,128)(2,1)}, u32[]{:S(2)}, u32[]{:S(2)}) async-start(bf16[64,6,3584]{2,1,0:T(8,128)(2,1)} %all_to_all.35), calls=%async_computation.1 | async-start | bytes 7340032 | tf_op jit(solution)/shard_map/all_to_all | solution.py:56
  148.2 84.5 %all-to-all-done.1 = bf16[64,6,3584]{2,1,0:T(8,128)(2,1)} async-done(((bf16[64,6,3584]{2,1,0:T(8,128)(2,1)}), bf16[64,6,3584]{2,1,0:T(8,128)(2,1)}, u32[]{:S(2)}, u32[]{:S(2)}) %all-to-all-start.1) | async-done | bytes 2752544 | tf_op jit(solution)/shard_map/all_to_all | solution.py:56
  232.7 5.5 %all_to_all.37 = bf16[384,3584]{1,0:T(8,128)(2,1)} reshape(bf16[64,6,3584]{2,1,0:T(8,128)(2,1)} %all-to-all-done.1) | data formatting | bytes 5505024 | tf_op jit(solution)/shard_map/all_to_all | solution.py:56
  238.2 2.7 fusion.5
  241.2 0.2 select_reduce_fusion
  241.4 0.3 fusion.4
  241.8 0.3 broadcast_in_dim.40
  242.1 90.3 %all_to_all.48 = bf16[64,6,3584]{2,1,0:T(8,128)(2,1)} all-to-all(bf16[64,6,3584]{2,1,0:T(8,128)(2,1)S(1)} %bitcast.38), channel_id=1, replica_groups=mesh['dp'=8,'expert'=64] {'expert'}, dimensions={0} | all-to-all | bytes 5505024 | tf_op jit(solution)/shard_map/all_to_all | solution.py:57
  332.4 5.5 %all_to_all.40 = bf16[384,3584]{1,0:T(8,128)(2,1)} reshape(bf16[64,6,3584]{2,1,0:T(8,128)(2,1)} %all_to_all.48) | data formatting | bytes 5505024 | tf_op jit(solution)/shard_map/all_to_all | solution.py:57
  337.9 2.6 convolution_convert_fusion.1
  340.5 0.2 copy-done.8
  340.7 0.9 multiply_convert_fusion
  341.6 0.9 copy-done.3
  342.5 0.7 convolution_convert_fusion.3
  343.2 0.9 fusion.14
  344.1 0.7 convolution_convert_fusion.2
  344.8 0.5 copy-done.6
  345.2 2.4 fusion
  347.7 5.4 %all_to_all.41 = bf16[64,6,3584]{2,1,0:T(8,128)(2,1)} reshape(bf16[384,3584]{1,0:T(8,128)(2,1)} %fusion) | data formatting | bytes 5505024 | tf_op jit(solution)/shard_map/all_to_all | solution.py:89
  353.1 5.6 %all-to-all-start.3 = ((bf16[64,6,3584]{2,1,0:T(8,128)(2,1)}), bf16[64,6,3584]{2,1,0:T(8,128)(2,1)}, u32[]{:S(2)}, u32[]{:S(2)}) async-start(bf16[64,6,3584]{2,1,0:T(8,128)(2,1)} %all_to_all.41), calls=%async_computation.3 | async-start | bytes 7340032 | tf_op jit(solution)/shard_map/all_to_all | solution.py:89
  358.7 1.7 pad_maximum_fusion
  360.4 4.5 copy.35
  365.0 0.7 copy.31
  366.0 2.4 fusion.13
  368.5 3.4 fusion.1
  371.8 71.8 %all-to-all-done.3 = bf16[64,6,3584]{2,1,0:T(8,128)(2,1)} async-done(((bf16[64,6,3584]{2,1,0:T(8,128)(2,1)}), bf16[64,6,3584]{2,1,0:T(8,128)(2,1)}, u32[]{:S(2)}, u32[]{:S(2)}) %all-to-all-start.3) | async-done | bytes 2752544 | tf_op jit(solution)/shard_map/all_to_all | solution.py:89
  443.6 5.6 %all_to_all.43 = bf16[384,3584]{1,0:T(8,128)(2,1)} reshape(bf16[64,6,3584]{2,1,0:T(8,128)(2,1)} %all-to-all-done.3) | data formatting | bytes 5505024 | tf_op jit(solution)/shard_map/all_to_all | solution.py:89
  449.2 3.4 convolution_convert_fusion.4
  452.6 1.7 fusion.11
  (57 shorter events, 1.7 us)
Async XLA Ops:
  7.2 231.1 %copy-start = (bf16[128,3584]{1,0:T(8,128)(2,1)S(1)}, bf16[128,3584]{1,0:T(8,128)(2,1)}, u32[]{:S(2)}) copy-start(bf16[128,3584]{1,0:T(8,128)(2,1)} %param.8) | copy-start | bytes 2752516
  16.6 2.9 copy-start.9
  22.0 11.0 %copy-start.10 = (bf16[448,128]{1,0:T(8,128)(2,1)S(1)}, bf16[448,128]{1,0:T(8,128)(2,1)}, u32[]{:S(2)}) copy-start(bf16[448,128]{1,0:T(8,128)(2,1)} %param.11) | copy-start | bytes 344068
  22.0 43.2 %copy-start.11 = (bf16[448,128]{1,0:T(8,128)(2,1)S(1)}, bf16[448,128]{1,0:T(8,128)(2,1)}, u32[]{:S(2)}) copy-start(bf16[448,128]{1,0:T(8,128)(2,1)} %param.12) | copy-start | bytes 344068
  22.1 69.8 %copy-start.12 = (bf16[448,128]{1,0:T(8,128)(2,1)S(1)}, bf16[448,128]{1,0:T(8,128)(2,1)}, u32[]{:S(2)}) copy-start(bf16[448,128]{1,0:T(8,128)(2,1)} %param.13) | copy-start | bytes 344068
  22.1 98.3 %all-to-all-start = ((bf16[64,6,3584]{2,1,0:T(8,128)(2,1)}), bf16[64,6,3584]{2,1,0:T(8,128)(2,1)}, u32[]{:S(2)}, u32[]{:S(2)}) async-start(bf16[64,6,3584]{2,1,0:T(8,128)(2,1)} %bitcast.37), calls=%async_computation | async-start | bytes 7340032 | tf_op jit(solution)/shard_map/all_to_all | solution.py:44
  91.8 36.8 %copy-start.5 = (bf16[3584,128]{1,0:T(8,128)(2,1)}, bf16[3584,128]{1,0:T(8,128)(2,1)S(1)}, u32[]{:S(2)}) copy-start(bf16[3584,128]{1,0:T(8,128)(2,1)S(1)} %all_gather.10) | copy-start | bytes 2752516
  125.8 2.8 copy-start.2
  128.7 1.2 copy-start.7
  137.7 10.1 %copy-start.13 = (f32[128,8]{0,1:T(8,128)S(1)}, f32[128,8]{0,1:T(8,128)}, u32[]{:S(2)}) copy-start(f32[128,8]{0,1:T(8,128)} %param.10) | copy-start | bytes 12292
  137.7 95.0 %all-to-all-start.1 = ((bf16[64,6,3584]{2,1,0:T(8,128)(2,1)}), bf16[64,6,3584]{2,1,0:T(8,128)(2,1)}, u32[]{:S(2)}, u32[]{:S(2)}) async-start(bf16[64,6,3584]{2,1,0:T(8,128)(2,1)} %all_to_all.35), calls=%async_computation.1 | async-start | bytes 7340032 | tf_op jit(solution)/shard_map/all_to_all | solution.py:56
  337.8 2.6 copy-start.4
  337.9 2.8 copy-start.8
  340.7 1.8 copy-start.3
  344.0 1.2 copy-start.6
  353.1 90.6 %all-to-all-start.3 = ((bf16[64,6,3584]{2,1,0:T(8,128)(2,1)}), bf16[64,6,3584]{2,1,0:T(8,128)(2,1)}, u32[]{:S(2)}, u32[]{:S(2)}) async-start(bf16[64,6,3584]{2,1,0:T(8,128)(2,1)} %all_to_all.41), calls=%async_computation.3 | async-start | bytes 7340032 | tf_op jit(solution)/shard_map/all_to_all | solution.py:89
  358.7 93.9 %reduce-scatter.4.cloned.1.call-start = ((), (), s32[]{:S(2)}) async-start(), calls=%async_computation.5 | async-start | bytes 3096576
  443.6 10.7 %copy-start.1 = (bf16[128,3584]{1,0:T(8,128)(2,1)S(1)}, bf16[128,3584]{1,0:T(8,128)(2,1)}, u32[]{:S(2)}) copy-start(bf16[128,3584]{1,0:T(8,128)(2,1)} %param.8) | copy-start | bytes 2752516
Sparse Core Ops, SparseCore 0:
  365.1 46.6 reduce-scatter.3
where the time goes:
time: 463 us; the launch traced here: 461 us
  blocking collectives  178 us (38%)
  waiting for transfers between devices  156 us (34%)
  local copies, waits for them, and re-layouts  51.9 us (11%)
  matrix products  26.8 us (6%)
  starting transfers between devices  26.8 us (6%)
  between operations  14.4 us (3%)
  other arithmetic  7.41 us (2%)
    all_to_all x1, blocking collectives, shards(): lax.all_to_all(spread(scaled_slots), 'expert', split_axis=0, concat_axis=...  90.3 us
    all_to_all x1, waiting for transfers between devices, shards(): lax.all_to_all(out_part, 'expert', split_axis=0, concat_axis=0, tiled=True)  84.5 us
    all_to_all x1, waiting for transfers between devices, shards(): lax.all_to_all(dx_part, 'expert', split_axis=0, concat_axis=0, tiled=True)  71.8 us
    all_gather x1, blocking collectives, shards(): lax.all_gather(gate_w, 'dp', axis=0, tiled=True)  32.2 us
    all_gather x1, blocking collectives, shards(): lax.all_gather(down_w, 'dp', axis=0, tiled=True)  28.6 us
    all_gather x1, blocking collectives, shards(): lax.all_gather(up_w, 'dp', axis=0, tiled=True)  26.5 us
    all_to_all x1, starting transfers between devices, shards(): lax.all_to_all(spread(token_slots), 'expert', split_axis=0, concat_axis=0...  11 us
    all_to_all x2, local copies, waits for them, and re-layouts, shards(): lax.all_to_all(dx_part, 'expert', split_axis=0, concat_axis=0, tiled=True)  11 us
  transfers between devices with their start and end apart: 4, of which 2 were waited for; matrix products, arithmetic and copies ran while one was open for 4% of the time, Pallas kernels for 0%

commit v1 on v0

--- a/solution.py
+++ b/solution.py
@@ -6,6 +6,12 @@
 TOP = 8
 SLICES = 8
 CAP = 6
+
+
+def gather_by_exchange(x, axis, dim):
+    size = lax.axis_size(axis)
+    repeats = [size if d == dim else 1 for d in range(x.ndim)]
+    return lax.all_to_all(jnp.tile(x, repeats), axis, split_axis=dim, concat_axis=dim, tiled=True)
 
 
 def shards(tokens, cotangent, route_ids, route_gates, gate_w, up_w, down_w):
@@ -38,7 +44,7 @@
 
     w_gate, w_up, w_down = (
         lax.all_gather(gate_w, "dp", axis=0, tiled=True),
-        lax.all_gather(up_w, "dp", axis=0, tiled=True),
+        gather_by_exchange(up_w, "dp", 0),
         lax.all_gather(down_w, "dp", axis=0, tiled=True),
     )
     token_rows = lax.all_to_all(

time: 463 us -> 539 us (1.16)
  blocking collectives: 178 us -> 258 us
    all_to_all x0 -> x1, blocking collectives: none -> 95.7 us  [shards(): lax.all_to_all(spread(token_slots), 'expert', split_axis=0, concat_axis=0...]
    all_gather x1 -> x0, blocking collectives: 26.5 us -> none  [shards(): lax.all_gather(up_w, 'dp', axis=0, tiled=True)]
    all_gather x1, blocking collectives: 32.2 us -> 43.4 us  [shards(): lax.all_gather(gate_w, 'dp', axis=0, tiled=True)]
where the time goes in v1:
time: 539 us; the launch traced here: 538 us
  blocking collectives  258 us (48%)
  waiting for transfers between devices  156 us (29%)
  local copies, waits for them, and re-layouts  50.9 us (9%)
  matrix products  28.8 us (5%)
  starting transfers between devices  22.3 us (4%)
  between operations  14.4 us (3%)
  other arithmetic  7.41 us (1%)
    all_to_all x1, blocking collectives, shards(): lax.all_to_all(spread(token_slots), 'expert', split_axis=0, concat_axis=0...  95.7 us
    all_to_all x1, blocking collectives, shards(): lax.all_to_all(spread(scaled_slots), 'expert', split_axis=0, concat_axis=...  90.3 us
    all_to_all x1, waiting for transfers between devices, shards(): lax.all_to_all(out_part, 'expert', split_axis=0, concat_axis=0, tiled=True)  84.5 us
    all_to_all x1, waiting for transfers between devices, shards(): lax.all_to_all(dx_part, 'expert', split_axis=0, concat_axis=0, tiled=True)  71.8 us
    all_gather x1, blocking collectives, shards(): lax.all_gather(gate_w, 'dp', axis=0, tiled=True)  43.4 us
    all_gather x1, blocking collectives, shards(): lax.all_gather(down_w, 'dp', axis=0, tiled=True)  28.4 us
    all_to_all x2, local copies, waits for them, and re-layouts, shards(): lax.all_to_all(dx_part, 'expert', split_axis=0, concat_axis=0, tiled=True)  11 us
    all_to_all x2, local copies, waits for them, and re-layouts, shards(): lax.all_to_all(out_part, 'expert', split_axis=0, concat_axis=0, tiled=True)  10.9 us
  transfers between devices with their start and end apart: 4, of which 2 were waited for; matrix products, arithmetic and copies ran while one was open for 4% of the time, Pallas kernels for 0%

profile of v1, /device:TPU:2, one launch (start us, length us, event | category | flops | bytes accessed | tf_op | source)
XLA Modules:
  0.0 537.8 jit_solution(5529414110759231997)
XLA Ops:
  7.2 0.9 copy.27
  8.4 2.3 reduce-window.6
  10.6 0.3 slice_reduce_fusion
  10.9 0.2 reduce-window.9
  11.2 1.9 and.18
  13.2 3.4 eq.81
  16.6 2.9 convert_reduce_fusion
  19.6 0.3 convolution_convert_fusion.6
  20.0 0.3 broadcast_in_dim.36
  20.2 95.7 %all_to_all.57 = bf16[64,6,3584]{2,1,0:T(8,128)(2,1)} all-to-all(bf16[64,6,3584]{2,1,0:T(8,128)(2,1)S(1)} %bitcast.38), channel_id=1, replica_groups=mesh['dp'=8,'expert'=64] {'expert'}, dimensions={0} | all-to-all | bytes 5505024 | tf_op jit(solution)/shard_map/all_to_all | solution.py:50
  115.9 1.0 tile.2
  116.9 10.3 %all-to-all-start.1 = ((bf16[8,448,128]{2,1,0:T(8,128)(2,1)}), bf16[8,448,128]{2,1,0:T(8,128)(2,1)S(1)}, u32[]{:S(2)}, u32[]{:S(2)}) async-start(bf16[8,448,128]{2,1,0:T(8,128)(2,1)} %tile.2), calls=%async_computation.1 | async-start | bytes 1835008 | tf_op jit(solution)/shard_map/all_to_all | solution.py:14
  127.3 43.4 %all_gather.6 = bf16[3584,128]{1,0:T(8,128)(2,1)S(1)} all-gather(bf16[448,128]{1,0:T(8,128)(2,1)S(1)} %copy-done.10), channel_id=1, replica_groups=mesh['dp'=8,'expert'=64] {'dp'}, dimensions={0}, use_global_device_ids=true | all-gather | bytes 1032192 | tf_op jit(solution)/shard_map/all_gather | solution.py:46
  170.7 28.4 %all_gather.7 = bf16[3584,128]{1,0:T(8,128)(2,1)} all-gather(bf16[448,128]{1,0:T(8,128)(2,1)S(1)} %copy-done.11), channel_id=1, replica_groups=mesh['dp'=8,'expert'=64] {'dp'}, dimensions={0}, use_global_device_ids=true | all-gather | bytes 1032192 | tf_op jit(solution)/shard_map/all_gather | solution.py:48
  199.1 5.5 %all_to_all.40 = bf16[384,3584]{1,0:T(8,128)(2,1)} reshape(bf16[64,6,3584]{2,1,0:T(8,128)(2,1)} %all_to_all.57) | data formatting | bytes 5505024 | tf_op jit(solution)/shard_map/all_to_all | solution.py:50
  204.5 2.6 fusion.12
  207.2 3.0 multiply_convert_fusion.2
  210.2 2.5 convolution_convert_fusion
  212.7 5.4 %all_to_all.43 = bf16[64,6,3584]{2,1,0:T(8,128)(2,1)} reshape(bf16[384,3584]{1,0:T(8,128)(2,1)} %convolution_convert_fusion) | data formatting | bytes 5505024 | tf_op jit(solution)/shard_map/all_to_all | solution.py:62
  218.1 6.4 %all-to-all-start.2 = ((bf16[64,6,3584]{2,1,0:T(8,128)(2,1)}), bf16[64,6,3584]{2,1,0:T(8,128)(2,1)}, u32[]{:S(2)}, u32[]{:S(2)}) async-start(bf16[64,6,3584]{2,1,0:T(8,128)(2,1)} %all_to_all.43), calls=%async_computation.2 | async-start | bytes 7340032 | tf_op jit(solution)/shard_map/all_to_all | solution.py:62
  224.9 84.5 %all-to-all-done.2 = bf16[64,6,3584]{2,1,0:T(8,128)(2,1)} async-done(((bf16[64,6,3584]{2,1,0:T(8,128)(2,1)}), bf16[64,6,3584]{2,1,0:T(8,128)(2,1)}, u32[]{:S(2)}, u32[]{:S(2)}) %all-to-all-start.2) | async-done | bytes 2752544 | tf_op jit(solution)/shard_map/all_to_all | solution.py:62
  309.4 5.5 %all_to_all.45 = bf16[384,3584]{1,0:T(8,128)(2,1)} reshape(bf16[64,6,3584]{2,1,0:T(8,128)(2,1)} %all-to-all-done.2) | data formatting | bytes 5505024 | tf_op jit(solution)/shard_map/all_to_all | solution.py:62
  314.9 2.7 fusion.5
  317.8 0.2 select_reduce_fusion
  318.1 0.3 fusion.4
  318.5 0.3 broadcast_in_dim.40
  318.7 90.3 %all_to_all.58 = bf16[64,6,3584]{2,1,0:T(8,128)(2,1)} all-to-all(bf16[64,6,3584]{2,1,0:T(8,128)(2,1)S(1)} %bitcast.39), channel_id=1, replica_groups=mesh['dp'=8,'expert'=64] {'expert'}, dimensions={0} | all-to-all | bytes 5505024 | tf_op jit(solution)/shard_map/all_to_all | solution.py:63
  409.0 5.5 %all_to_all.48 = bf16[384,3584]{1,0:T(8,128)(2,1)} reshape(bf16[64,6,3584]{2,1,0:T(8,128)(2,1)} %all_to_all.58) | data formatting | bytes 5505024 | tf_op jit(solution)/shard_map/all_to_all | solution.py:63
  414.5 2.6 convolution_convert_fusion.1
  417.1 0.2 copy-done.7
  417.3 0.9 multiply_convert_fusion
  418.2 0.9 copy-done.2
  419.1 0.7 convolution_convert_fusion.3
  419.8 0.9 fusion.14
  420.7 0.7 convolution_convert_fusion.2
  421.4 0.5 copy-done.5
  421.9 2.4 fusion
  424.3 5.4 %all_to_all.49 = bf16[64,6,3584]{2,1,0:T(8,128)(2,1)} reshape(bf16[384,3584]{1,0:T(8,128)(2,1)} %fusion) | data formatting | bytes 5505024 | tf_op jit(solution)/shard_map/all_to_all | solution.py:95
  429.7 5.6 %all-to-all-start.4 = ((bf16[64,6,3584]{2,1,0:T(8,128)(2,1)}), bf16[64,6,3584]{2,1,0:T(8,128)(2,1)}, u32[]{:S(2)}, u32[]{:S(2)}) async-start(bf16[64,6,3584]{2,1,0:T(8,128)(2,1)} %all_to_all.49), calls=%async_computation.4 | async-start | bytes 7340032 | tf_op jit(solution)/shard_map/all_to_all | solution.py:95
  435.4 1.7 pad_maximum_fusion
  437.1 4.5 copy.35
  441.7 0.7 copy.31
  442.7 2.4 fusion.13
  445.2 3.4 fusion.1
  448.5 71.8 %all-to-all-done.4 = bf16[64,6,3584]{2,1,0:T(8,128)(2,1)} async-done(((bf16[64,6,3584]{2,1,0:T(8,128)(2,1)}), bf16[64,6,3584]{2,1,0:T(8,128)(2,1)}, u32[]{:S(2)}, u32[]{:S(2)}) %all-to-all-start.4) | async-done | bytes 2752544 | tf_op jit(solution)/shard_map/all_to_all | solution.py:95
  520.3 5.6 %all_to_all.51 = bf16[384,3584]{1,0:T(8,128)(2,1)} reshape(bf16[64,6,3584]{2,1,0:T(8,128)(2,1)} %all-to-all-done.4) | data formatting | bytes 5505024 | tf_op jit(solution)/shard_map/all_to_all | solution.py:95
  525.9 3.4 convolution_convert_fusion.4
  529.2 1.7 fusion.11
  (56 shorter events, 1.7 us)
Async XLA Ops:
  7.2 307.7 %copy-start = (bf16[128,3584]{1,0:T(8,128)(2,1)S(1)}, bf16[128,3584]{1,0:T(8,128)(2,1)}, u32[]{:S(2)}) copy-start(bf16[128,3584]{1,0:T(8,128)(2,1)} %param.8) | copy-start | bytes 2752516
  16.6 2.9 copy-start.8
  20.2 95.7 %copy-start.9 = (bf16[448,128]{1,0:T(8,128)(2,1)S(1)}, bf16[448,128]{1,0:T(8,128)(2,1)}, u32[]{:S(2)}) copy-start(bf16[448,128]{1,0:T(8,128)(2,1)} %param.12) | copy-start | bytes 344068
  115.9 11.4 %copy-start.10 = (bf16[448,128]{1,0:T(8,128)(2,1)S(1)}, bf16[448,128]{1,0:T(8,128)(2,1)}, u32[]{:S(2)}) copy-start(bf16[448,128]{1,0:T(8,128)(2,1)} %param.11) | copy-start | bytes 344068
  115.9 54.8 %copy-start.11 = (bf16[448,128]{1,0:T(8,128)(2,1)S(1)}, bf16[448,128]{1,0:T(8,128)(2,1)}, u32[]{:S(2)}) copy-start(bf16[448,128]{1,0:T(8,128)(2,1)} %param.13) | copy-start | bytes 344068
  116.9 90.2 %all-to-all-start.1 = ((bf16[8,448,128]{2,1,0:T(8,128)(2,1)}), bf16[8,448,128]{2,1,0:T(8,128)(2,1)S(1)}, u32[]{:S(2)}, u32[]{:S(2)}) async-start(bf16[8,448,128]{2,1,0:T(8,128)(2,1)} %tile.2), calls=%async_computation.1 | async-start | bytes 1835008 | tf_op jit(solution)/shard_map/all_to_all | solution.py:14
  207.2 3.0 copy-start.4
  207.2 3.0 copy-start.6
  218.1 6.4 %copy-start.12 = (f32[128,8]{0,1:T(8,128)S(1)}, f32[128,8]{0,1:T(8,128)}, u32[]{:S(2)}) copy-start(f32[128,8]{0,1:T(8,128)} %param.10) | copy-start | bytes 12292
  218.1 91.3 %all-to-all-start.2 = ((bf16[64,6,3584]{2,1,0:T(8,128)(2,1)}), bf16[64,6,3584]{2,1,0:T(8,128)(2,1)}, u32[]{:S(2)}, u32[]{:S(2)}) async-start(bf16[64,6,3584]{2,1,0:T(8,128)(2,1)} %all_to_all.43), calls=%async_computation.2 | async-start | bytes 7340032 | tf_op jit(solution)/shard_map/all_to_all | solution.py:62
  414.5 2.6 copy-start.3
  414.5 2.8 copy-start.7
  417.3 1.8 copy-start.2
  420.7 1.2 copy-start.5
  429.7 90.6 %all-to-all-start.4 = ((bf16[64,6,3584]{2,1,0:T(8,128)(2,1)}), bf16[64,6,3584]{2,1,0:T(8,128)(2,1)}, u32[]{:S(2)}, u32[]{:S(2)}) async-start(bf16[64,6,3584]{2,1,0:T(8,128)(2,1)} %all_to_all.49), calls=%async_computation.4 | async-start | bytes 7340032 | tf_op jit(solution)/shard_map/all_to_all | solution.py:95
  435.3 93.9 %reduce-scatter.4.cloned.1.call-start = ((), (), s32[]{:S(2)}) async-start(), calls=%async_computation.6 | async-start | bytes 3096576
  520.3 10.7 %copy-start.1 = (bf16[128,3584]{1,0:T(8,128)(2,1)S(1)}, bf16[128,3584]{1,0:T(8,128)(2,1)}, u32[]{:S(2)}) copy-start(bf16[128,3584]{1,0:T(8,128)(2,1)} %param.8) | copy-start | bytes 2752516
Sparse Core Ops, SparseCore 0:
  441.8 47.6 reduce-scatter.3
